TPU v7x, 32 devices: a whole 2x2x4 slice. The times are simulated.
32 devices in a mesh: node: 4 (over z), dom: 8 (over y, x, core).
Axes of the slice: x: 2, y: 2, z: 4, core: 2. Of those that a mesh axis runs over, the one named last changes fastest.
Arguments:
- probes: float32 [32, 16, 16, 128], P(None, 'dom'), may hold values from -24 to 24
- slope: float32 [16, 16, 128], P('dom'), may hold values from 4 to 6
- root: float32 [16, 16, 128], P('dom'), may hold values from 0.3 to 0.7
- damping: float32 [16, 16, 128], P('dom'), may hold values from 0.3 to 1.2
Outputs:
- moments: float32 [2, 2, 32, 16, 16, 128], P(None, None, 'node', 'dom')
- projections: float32 [2, 2, 32, 32], replicated
All inputs are finite; a program needn't handle non-finite values.
Results may differ from a plain program's by a relative error of at most 0.00013.
Values sent between devices are 32-bit elements; how exact they have to be, the bound alone decides.
A program may use at most 64 MiB of HBM per device.

v0:
```python
import math
import jax
import jax.numpy as jnp
from jax import lax
from jax.sharding import PartitionSpec as P

NODE_DEV = 2
SWEEPS = 8
CENTRE = 0.5
RADIUS = 2.0


def grid_step(source, fields, factor_re, factor_im):
    padded = jnp.pad(fields, ((0, 0), (0, 0), (1, 1), (1, 1), (1, 1)))
    total = padded[:, :, 2:, 1:-1, 1:-1] + padded[:, :, :-2, 1:-1, 1:-1]
    total = total + padded[:, :, 1:-1, 2:, 1:-1] + padded[:, :, 1:-1, :-2, 1:-1]
    total = total + padded[:, :, 1:-1, 1:-1, 2:] + padded[:, :, 1:-1, 1:-1, :-2]
    real_part = source + total[:, 0]
    imag_part = total[:, 1]
    return jnp.stack(
        [
            real_part * factor_re - imag_part * factor_im,
            real_part * factor_im + imag_part * factor_re,
        ],
        axis=1,
    )


def inverse_diagonal(shift_real, shift_imaginary, slope, root, damping, guard):
    zr_col = shift_real[:, None, None, None, None]
    zi_col = shift_imaginary[:, None, None, None, None]
    decay = jnp.exp(-zr_col)
    real_d = slope * (zr_col - root) + damping * (decay * jnp.cos(zi_col))
    imag_d = slope * zi_col - damping * (decay * jnp.sin(zi_col))
    scale = 1.0 / (real_d * real_d + imag_d * imag_d + guard)
    return (real_d * scale, -imag_d * scale)


def per_system(fields, weight_re, weight_im):
    a_col = weight_re[:, None, None, None]
    b_col = weight_im[:, None, None, None]
    return jnp.stack(
        [a_col * fields[:, 0] - b_col * fields[:, 1], a_col * fields[:, 1] + b_col * fields[:, 0]]
    )


def body(probes, slope, root, damping):
    vectors = probes.shape[0]
    planes = probes.shape[1]
    groups = lax.axis_size("node")
    total = NODE_DEV * groups
    first = (lax.axis_index("node") * NODE_DEV).astype(jnp.float32)
    dom_size = lax.axis_size("dom")
    count = NODE_DEV * vectors // dom_size
    replicated = jnp.broadcast_to(probes[None], (NODE_DEV,) + probes.shape).reshape(
        (NODE_DEV * vectors,) + probes.shape[1:]
    )
    own = lax.all_to_all(replicated, "dom", split_axis=0, concat_axis=1, tiled=True)
    slope_all, root_all, damping_all = (
        lax.all_gather(slope, "dom", axis=0, tiled=True),
        lax.all_gather(root, "dom", axis=0, tiled=True),
        lax.all_gather(damping, "dom", axis=0, tiled=True),
    )
    system = lax.axis_index("dom") * count + jnp.arange(count)
    position = first + (system // vectors).astype(jnp.float32)
    theta = 2.0 * math.pi * (position + 0.5) / total
    shift_real = CENTRE + RADIUS * jnp.cos(theta)
    shift_imaginary = RADIUS * jnp.sin(theta)
    qre, qim = inverse_diagonal(
        shift_real, shift_imaginary, slope_all[None], root_all[None], damping_all[None], 0.0
    )
    qre = qre[:, 0]
    qim = qim[:, 0]
    fields = jnp.stack([own * qre, own * qim], axis=1)
    for sweep in range(SWEEPS):
        fields = grid_step(own, fields, qre, qim)
    weight_re = RADIUS * jnp.cos(theta) / total
    weight_im = RADIUS * jnp.sin(theta) / total
    shifted_re = weight_re * shift_real - weight_im * shift_imaginary
    shifted_im = weight_re * shift_imaginary + weight_im * shift_real
    terms = jnp.stack(
        [per_system(fields, weight_re, weight_im), per_system(fields, shifted_re, shifted_im)]
    )
    back = lax.all_to_all(terms, "dom", split_axis=3, concat_axis=2, tiled=True)
    local = jnp.sum(back.reshape((2, 2, NODE_DEV, vectors) + probes.shape[1:]), axis=2)
    flat = local.reshape(4 * vectors, -1)
    basis = probes.reshape(vectors, -1)
    partial_value = lax.dot_general(
        flat,
        basis,
        (((1,), (1,)), ((), ())),
        precision=lax.Precision.HIGHEST,
        preferred_element_type=jnp.float32,
    )
    cells = planes * probes.shape[2] * probes.shape[3] * lax.axis_size("dom")
    projections = lax.psum(partial_value.reshape(2, 2, vectors, vectors) / cells, ("node", "dom"))
    summed = lax.psum(local, "node")
    share = vectors // groups
    moments = lax.dynamic_slice_in_dim(summed, lax.axis_index("node") * share, share, 2)
    return (moments, projections)


def solution(mesh):
    in_specs = (
        P(None, "dom", None, None),
        P("dom", None, None),
        P("dom", None, None),
        P("dom", None, None),
    )
    out_specs = (P(None, None, "node", "dom", None, None), P())
    return jax.shard_map(body, mesh=mesh, in_specs=in_specs, out_specs=out_specs, check_vma=False)
```

profile of v0, /device:TPU:0, one launch (start us, length us, event | category | flops | bytes accessed | tf_op | source)
XLA Modules:
  0.0 260.8 jit_solution(6893673430703613702)
XLA Ops:
  7.2 2.2 broadcast_in_dim.2
  9.4 5.2 %all-to-all-start = ((f32[64,2,16,128]{3,2,1,0:T(8,128)}), f32[64,2,16,128]{3,2,1,0:T(8,128)S(1)}, u32[]{:S(2)}, u32[]{:S(2)}) async-start(f32[64,2,16,128]{3,2,1,0:T(8,128)} %bitcast), calls=%async_computation | async-start | bytes 2097152 | tf_op jit(solution)/shard_map/all_to_all | solution.py:58
  14.6 18.8 %all_gather.9 = f32[16,16,128]{2,1,0:T(8,128)S(1)} all-gather(f32[2,16,128]{2,1,0:T(8,128)S(1)} %copy-done.2), channel_id=1, replica_groups=mesh['node'=4,'dom'=8] {'dom'}, dimensions={0}, use_global_device_ids=true | all-gather | bytes 147456 | tf_op jit(solution)/shard_map/all_gather | solution.py:60
  33.4 8.3 %all_gather.10 = f32[16,16,128]{2,1,0:T(8,128)S(1)} all-gather(f32[2,16,128]{2,1,0:T(8,128)S(1)} %copy-done.3), channel_id=1, replica_groups=mesh['node'=4,'dom'=8] {'dom'}, dimensions={0}, use_global_device_ids=true | all-gather | bytes 147456 | tf_op jit(solution)/shard_map/all_gather | solution.py:61
  41.7 9.1 %all_gather.11 = f32[16,16,128]{2,1,0:T(8,128)S(1)} all-gather(f32[2,16,128]{2,1,0:T(8,128)S(1)} %copy-done.4), channel_id=1, replica_groups=mesh['node'=4,'dom'=8] {'dom'}, dimensions={0}, use_global_device_ids=true | all-gather | bytes 147456 | tf_op jit(solution)/shard_map/all_gather | solution.py:62
  50.8 0.1 multiply_subtract_fusion.12
  50.9 0.0 all-to-all-done
  50.9 0.1 copy.15
  51.0 0.6 fusion.19
  51.6 2.6 select_maximum_fusion.7
  54.2 3.3 %slice_add_fusion.35 = f32[8,2,16,16,128]{4,3,2,0,1:T(8,128)S(1)} fusion(f32[8,2,18,18,130]{4,3,2,0,1:T(8,128)S(1)} %select_maximum_fusion.7), kind=kLoop, calls=%fused_computation.56 | loop fusion | flops 2621440 | bytes 14680064 | tf_op jit(solution)/shard_map/add | solution.py:17
  57.5 0.8 multiply_subtract_fusion.10
  58.3 2.4 select_maximum_fusion.6
  60.7 3.3 %slice_add_fusion.30 = f32[8,2,16,16,128]{4,3,2,0,1:T(8,128)S(1)} fusion(f32[8,2,18,18,130]{4,3,2,0,1:T(8,128)S(1)} %select_maximum_fusion.6), kind=kLoop, calls=%fused_computation.51 | loop fusion | flops 2621440 | bytes 14680064 | tf_op jit(solution)/shard_map/add | solution.py:17
  63.9 0.8 multiply_subtract_fusion.9
  64.7 2.4 select_maximum_fusion.5
  67.1 3.3 %slice_add_fusion.25 = f32[8,2,16,16,128]{4,3,2,0,1:T(8,128)S(1)} fusion(f32[8,2,18,18,130]{4,3,2,0,1:T(8,128)S(1)} %select_maximum_fusion.5), kind=kLoop, calls=%fused_computation.46 | loop fusion | flops 2621440 | bytes 14680064 | tf_op jit(solution)/shard_map/add | solution.py:17
  70.4 0.8 multiply_subtract_fusion.8
  71.2 2.4 select_maximum_fusion.4
  73.6 3.3 %slice_add_fusion.20 = f32[8,2,16,16,128]{4,3,2,0,1:T(8,128)S(1)} fusion(f32[8,2,18,18,130]{4,3,2,0,1:T(8,128)S(1)} %select_maximum_fusion.4), kind=kLoop, calls=%fused_computation.41 | loop fusion | flops 2621440 | bytes 14680064 | tf_op jit(solution)/shard_map/add | solution.py:17
  76.8 0.8 multiply_subtract_fusion.7
  77.6 2.6 select_maximum_fusion.3
  80.2 3.3 %slice_add_fusion.15 = f32[8,2,16,16,128]{4,3,2,0,1:T(8,128)S(1)} fusion(f32[8,2,18,18,130]{4,3,2,0,1:T(8,128)S(1)} %select_maximum_fusion.3), kind=kLoop, calls=%fused_computation.36 | loop fusion | flops 2621440 | bytes 14680064 | tf_op jit(solution)/shard_map/add | solution.py:17
  83.5 0.8 multiply_subtract_fusion.6
  84.3 2.4 select_maximum_fusion.2
  86.7 3.3 %slice_add_fusion.10 = f32[8,2,16,16,128]{4,3,2,0,1:T(8,128)S(1)} fusion(f32[8,2,18,18,130]{4,3,2,0,1:T(8,128)S(1)} %select_maximum_fusion.2), kind=kLoop, calls=%fused_computation.31 | loop fusion | flops 2621440 | bytes 14680064 | tf_op jit(solution)/shard_map/add | solution.py:17
  90.0 0.8 multiply_subtract_fusion.5
  90.8 2.4 select_maximum_fusion.1
  93.1 3.3 %slice_add_fusion.5 = f32[8,2,16,16,128]{4,3,2,0,1:T(8,128)S(1)} fusion(f32[8,2,18,18,130]{4,3,2,0,1:T(8,128)S(1)} %select_maximum_fusion.1), kind=kLoop, calls=%fused_computation.26 | loop fusion | flops 2621440 | bytes 14680064 | tf_op jit(solution)/shard_map/add | solution.py:17
  96.4 0.8 multiply_subtract_fusion.4
  97.2 2.4 select_maximum_fusion
  99.6 3.5 %slice_add_fusion = f32[8,2,16,16,128]{4,3,2,0,1:T(8,128)S(1)} fusion(f32[8,2,18,18,130]{4,3,2,0,1:T(8,128)S(1)} %select_maximum_fusion), kind=kLoop, calls=%fused_computation.21 | loop fusion | flops 2621440 | bytes 14680064 | tf_op jit(solution)/shard_map/add | solution.py:17
  103.1 0.9 multiply_subtract_fusion.1
  104.1 0.5 multiply_subtract_fusion
  104.6 0.4 maximum_bitcast_fusion
  105.0 0.4 pad_maximum_fusion
  105.4 0.6 copy.17
  106.0 51.6 %all_to_all.36 = f32[2,2,8,16,16,128]{5,4,2,1,0,3:T(8,128)S(1)} all-to-all(f32[2,2,8,16,16,128]{5,4,2,1,0,3:T(8,128)S(1)} %copy.17), channel_id=1, replica_groups=mesh['node'=4,'dom'=8] {'dom'}, dimensions={3} | all-to-all | bytes 8388608 | tf_op jit(solution)/shard_map/all_to_all | solution.py:84
  157.6 0.5 copy.19
  158.2 0.0 copy-start.1
  158.2 0.5 bitcast_reduce_fusion
  158.7 0.5 copy-done.1
  159.2 3.1 %fusion.10 = f32[2,2,32,32]{3,2,1,0:T(8,128)S(1)} fusion(f32[2,2,32,2,16,128]{5,4,3,2,1,0:T(8,128)S(1)} %bitcast_reduce_fusion, f32[32,2,16,128,1,1]{3,2,1,0,5,4:T(8,128)S(1)} %bitcast.53), kind=kOutput, calls=%fused_computation.66 | convolution fusion | flops 201330688 | bytes 2637824 | tf_op jit(solution)/shard_map/dot_general | solution.py:88
  162.3 0.0 all-reduce.10.cloned.1.call-start
  162.4 0.7 all-reduce.10.cloned.1.call-update
  163.1 42.9 %psum.15 = f32[2,2,32,32]{3,2,1,0:T(8,128)} all-reduce(f32[2,2,32,32]{3,2,1,0:T(8,128)S(1)} %fusion.10), channel_id=1, replica_groups=mesh['node'=4,'dom'=8] {'node','dom'}, use_global_device_ids=true, to_apply=%region_2.3 | all-reduce | flops 4096 | bytes 32768 | tf_op jit(solution)/shard_map/psum | solution.py:96
  206.0 46.1 %all-reduce.10.cloned.1.call-done = f32[2,2,32,2,16,128]{5,4,3,2,1,0:T(8,128)} async-done(((f32[2,2,32,2,16,128]{5,4,3,2,1,0:T(8,128)}), f32[2,2,32,2,16,128]{5,4,3,2,1,0:T(8,128)}) %all-reduce.10.cloned.1.call-update) | async-done | bytes 2097168 | tf_op jit(solution)/shard_map/psum | solution.py:97
  252.1 1.9 constant_dynamic-slice_fusion
  (9 shorter events, 0.1 us)
Async XLA Ops:
  7.2 7.4 %copy-start.2 = (f32[2,16,128]{2,1,0:T(8,128)S(1)}, f32[2,16,128]{2,1,0:T(8,128)}, u32[]{:S(2)}) copy-start(f32[2,16,128]{2,1,0:T(8,128)} %param.5) | copy-start | bytes 49156
  7.2 26.2 %copy-start.3 = (f32[2,16,128]{2,1,0:T(8,128)S(1)}, f32[2,16,128]{2,1,0:T(8,128)}, u32[]{:S(2)}) copy-start(f32[2,16,128]{2,1,0:T(8,128)} %param.6) | copy-start | bytes 49156
  7.2 34.5 %copy-start.4 = (f32[2,16,128]{2,1,0:T(8,128)S(1)}, f32[2,16,128]{2,1,0:T(8,128)}, u32[]{:S(2)}) copy-start(f32[2,16,128]{2,1,0:T(8,128)} %param.7) | copy-start | bytes 49156
  9.4 41.5 %all-to-all-start = ((f32[64,2,16,128]{3,2,1,0:T(8,128)}), f32[64,2,16,128]{3,2,1,0:T(8,128)S(1)}, u32[]{:S(2)}, u32[]{:S(2)}) async-start(f32[64,2,16,128]{3,2,1,0:T(8,128)} %bitcast), calls=%async_computation | async-start | bytes 2097152 | tf_op jit(solution)/shard_map/all_to_all | solution.py:58
  158.2 1.0 copy-start.1
  158.7 3.6 %copy-start = (f32[2,2,32,2,16,128]{5,4,3,2,1,0:T(8,128)}, f32[2,2,32,2,16,128]{5,4,3,2,1,0:T(8,128)S(1)}, u32[]{:S(2)}) copy-start(f32[2,2,32,2,16,128]{5,4,3,2,1,0:T(8,128)S(1)} %bitcast_reduce_fusion) | copy-start | bytes 6291460
  162.3 89.8 %all-reduce.10.cloned.1.call-start = ((), (), s32[]{:S(2)}) async-start(), calls=%async_computation.2 | async-start | bytes 4194304 | tf_op jit(solution)/shard_map/psum | solution.py:97
Sparse Core Ops, SparseCore 0:
  165.5 86.5 all-reduce.9
where the time goes:
time: 261 us
  blocking collectives  131 us (50%)
  other arithmetic  54.8 us (21%)
  waiting for transfers between devices  46.8 us (18%)
  between operations  14.3 us (5%)
  local copies, waits for them, and re-layouts  5.8 us (2%)
  starting transfers between devices  5.24 us (2%)
  matrix products  3.08 us (1%)
    all_to_all x1, blocking collectives, body(): back = lax.all_to_all(terms, 'dom', split_axis=3, concat_axis=2, tiled=True)  51.6 us
    psum x1, waiting for transfers between devices, body(): summed = lax.psum(local, 'node')  46.1 us
    psum x1, blocking collectives, body(): lax.psum(partial_value.reshape(2, 2, vectors, vectors) / cells, ('node',...  42.9 us
    add x8, other arithmetic, grid_step(): total = total + padded[:, :, 1:-1, 1:-1, 2:] + padded[:, :, 1:-1, 1:-1, :-2]  26.4 us
    all_gather x1, blocking collectives, body(): lax.all_gather(slope, 'dom', axis=0, tiled=True)  18.8 us
    another operation x7, other arithmetic, grid_step(): jnp.stack([real_part * factor_re - imag_part * factor_im, real_part * fac...  16.9 us
    all_gather x1, blocking collectives, body(): lax.all_gather(damping, 'dom', axis=0, tiled=True)  9.1 us
    all_gather x1, blocking collectives, body(): lax.all_gather(root, 'dom', axis=0, tiled=True)  8.31 us
  transfers between devices with their start and end apart: 2, of which 1 were waited for; matrix products, arithmetic and copies ran while one was open for 0% of the time, Pallas kernels for 0%

commit v1 on v0

--- a/solution.py
+++ b/solution.py
@@ -94,7 +94,9 @@
     )
     cells = planes * probes.shape[2] * probes.shape[3] * lax.axis_size("dom")
     projections = lax.psum(partial_value.reshape(2, 2, vectors, vectors) / cells, ("node", "dom"))
-    summed = lax.psum(local, "node")
+    summed = local
+    for hop in (1, 2):
+        summed = summed + lax.ppermute(summed, "node", [(dev, dev ^ hop) for dev in range(4)])
     share = vectors // groups
     moments = lax.dynamic_slice_in_dim(summed, lax.axis_index("node") * share, share, 2)
     return (moments, projections)

time: 261 us -> 318 us (1.22)
  blocking collectives: 131 us -> 196 us
  between operations: 14.3 us -> 0.93 us
  starting transfers between devices: 5.24 us -> 9.43 us
  other arithmetic: 54.8 us -> 58.8 us
    psum x1, blocking collectives: 42.9 us -> 108 us  [body(): lax.psum(partial_value.reshape(2, 2, vectors, vectors) / cells, ('node',...]
    psum x1 -> x0, waiting for transfers between devices: 46.1 us -> none  [body(): summed = lax.psum(local, 'node')]
    ppermute x0 -> x2, waiting for transfers between devices: none -> 45.2 us  [body(): lax.ppermute(summed, 'node', [(dev, dev ^ hop) for dev in range(4)])]
    ppermute x0 -> x2, starting transfers between devices: none -> 4.23 us  [body(): lax.ppermute(summed, 'node', [(dev, dev ^ hop) for dev in range(4)])]
    add x0 -> x2, other arithmetic: none -> 3.89 us  [body(): summed + lax.ppermute(summed, 'node', [(dev, dev ^ hop) for dev in range(...]
  transfers between devices with their start and end apart: 2 -> 3, of which waited for: 1 -> 1; matrix products, arithmetic and copies ran while one was open for 0% -> 1% of each run, Pallas kernels for 0% -> 0%
where the time goes in v1:
time: 318 us; the launch traced here: 317 us
  blocking collectives  196 us (62%)
  other arithmetic  58.8 us (18%)
  waiting for transfers between devices  45.2 us (14%)
  starting transfers between devices  9.43 us (3%)
  local copies, waits for them, and re-layouts  3.41 us (1%)
    psum x1, blocking collectives, body(): lax.psum(partial_value.reshape(2, 2, vectors, vectors) / cells, ('node',...  108 us
    all_to_all x1, blocking collectives, body(): back = lax.all_to_all(terms, 'dom', split_axis=3, concat_axis=2, tiled=True)  51.6 us
    ppermute x2, waiting for transfers between devices, body(): lax.ppermute(summed, 'node', [(dev, dev ^ hop) for dev in range(4)])  45.2 us
    add x8, other arithmetic, grid_step(): total = total + padded[:, :, 1:-1, 1:-1, 2:] + padded[:, :, 1:-1, 1:-1, :-2]  26.4 us
    all_gather x1, blocking collectives, body(): lax.all_gather(slope, 'dom', axis=0, tiled=True)  18.8 us
    another operation x7, other arithmetic, grid_step(): jnp.stack([real_part * factor_re - imag_part * factor_im, real_part * fac...  16.9 us
    all_gather x1, blocking collectives, body(): lax.all_gather(damping, 'dom', axis=0, tiled=True)  9.1 us
    all_gather x1, blocking collectives, body(): lax.all_gather(root, 'dom', axis=0, tiled=True)  8.31 us
  transfers between devices with their start and end apart: 3, of which 1 were waited for; matrix products, arithmetic and copies ran while one was open for 1% of the time, Pallas kernels for 0%

profile of v1, /device:TPU:0, one launch (start us, length us, event | category | flops | bytes accessed | tf_op | source)
XLA Modules:
  0.0 317.1 jit_solution(12712035526979914572)
XLA Ops:
  0.7 2.2 broadcast_in_dim.2
  2.8 5.2 %all-to-all-start = ((f32[64,2,16,128]{3,2,1,0:T(8,128)}), f32[64,2,16,128]{3,2,1,0:T(8,128)S(1)}, u32[]{:S(2)}, u32[]{:S(2)}) async-start(f32[64,2,16,128]{3,2,1,0:T(8,128)} %bitcast), calls=%async_computation | async-start | bytes 2097152 | tf_op jit(solution)/shard_map/all_to_all | solution.py:58
  8.0 18.8 %all_gather.9 = f32[16,16,128]{2,1,0:T(8,128)S(1)} all-gather(f32[2,16,128]{2,1,0:T(8,128)S(1)} %copy-done.1), channel_id=1, replica_groups=mesh['node'=4,'dom'=8] {'dom'}, dimensions={0}, use_global_device_ids=true | all-gather | bytes 147456 | tf_op jit(solution)/shard_map/all_gather | solution.py:60
  26.9 8.3 %all_gather.10 = f32[16,16,128]{2,1,0:T(8,128)S(1)} all-gather(f32[2,16,128]{2,1,0:T(8,128)S(1)} %copy-done.2), channel_id=1, replica_groups=mesh['node'=4,'dom'=8] {'dom'}, dimensions={0}, use_global_device_ids=true | all-gather | bytes 147456 | tf_op jit(solution)/shard_map/all_gather | solution.py:61
  35.2 9.1 %all_gather.11 = f32[16,16,128]{2,1,0:T(8,128)S(1)} all-gather(f32[2,16,128]{2,1,0:T(8,128)S(1)} %copy-done.3), channel_id=1, replica_groups=mesh['node'=4,'dom'=8] {'dom'}, dimensions={0}, use_global_device_ids=true | all-gather | bytes 147456 | tf_op jit(solution)/shard_map/all_gather | solution.py:62
  44.3 0.1 multiply_subtract_fusion.12
  44.4 0.1 copy.15
  44.5 0.6 fusion.19
  45.1 2.6 select_maximum_fusion.7
  47.7 3.3 %slice_add_fusion.35 = f32[8,2,16,16,128]{4,3,2,0,1:T(8,128)S(1)} fusion(f32[8,2,18,18,130]{4,3,2,0,1:T(8,128)S(1)} %select_maximum_fusion.7), kind=kLoop, calls=%fused_computation.56 | loop fusion | flops 2621440 | bytes 14680064 | tf_op jit(solution)/shard_map/add | solution.py:17
  50.9 0.8 multiply_subtract_fusion.10
  51.7 2.4 select_maximum_fusion.6
  54.1 3.3 %slice_add_fusion.30 = f32[8,2,16,16,128]{4,3,2,0,1:T(8,128)S(1)} fusion(f32[8,2,18,18,130]{4,3,2,0,1:T(8,128)S(1)} %select_maximum_fusion.6), kind=kLoop, calls=%fused_computation.51 | loop fusion | flops 2621440 | bytes 14680064 | tf_op jit(solution)/shard_map/add | solution.py:17
  57.4 0.8 multiply_subtract_fusion.9
  58.2 2.4 select_maximum_fusion.5
  60.6 3.3 %slice_add_fusion.25 = f32[8,2,16,16,128]{4,3,2,0,1:T(8,128)S(1)} fusion(f32[8,2,18,18,130]{4,3,2,0,1:T(8,128)S(1)} %select_maximum_fusion.5), kind=kLoop, calls=%fused_computation.46 | loop fusion | flops 2621440 | bytes 14680064 | tf_op jit(solution)/shard_map/add | solution.py:17
  63.8 0.8 multiply_subtract_fusion.8
  64.6 2.4 select_maximum_fusion.4
  67.0 3.3 %slice_add_fusion.20 = f32[8,2,16,16,128]{4,3,2,0,1:T(8,128)S(1)} fusion(f32[8,2,18,18,130]{4,3,2,0,1:T(8,128)S(1)} %select_maximum_fusion.4), kind=kLoop, calls=%fused_computation.41 | loop fusion | flops 2621440 | bytes 14680064 | tf_op jit(solution)/shard_map/add | solution.py:17
  70.3 0.8 multiply_subtract_fusion.7
  71.1 2.6 select_maximum_fusion.3
  73.7 3.3 %slice_add_fusion.15 = f32[8,2,16,16,128]{4,3,2,0,1:T(8,128)S(1)} fusion(f32[8,2,18,18,130]{4,3,2,0,1:T(8,128)S(1)} %select_maximum_fusion.3), kind=kLoop, calls=%fused_computation.36 | loop fusion | flops 2621440 | bytes 14680064 | tf_op jit(solution)/shard_map/add | solution.py:17
  77.0 0.8 multiply_subtract_fusion.6
  77.8 2.4 select_maximum_fusion.2
  80.1 3.3 %slice_add_fusion.10 = f32[8,2,16,16,128]{4,3,2,0,1:T(8,128)S(1)} fusion(f32[8,2,18,18,130]{4,3,2,0,1:T(8,128)S(1)} %select_maximum_fusion.2), kind=kLoop, calls=%fused_computation.31 | loop fusion | flops 2621440 | bytes 14680064 | tf_op jit(solution)/shard_map/add | solution.py:17
  83.4 0.8 multiply_subtract_fusion.5
  84.2 2.4 select_maximum_fusion.1
  86.6 3.3 %slice_add_fusion.5 = f32[8,2,16,16,128]{4,3,2,0,1:T(8,128)S(1)} fusion(f32[8,2,18,18,130]{4,3,2,0,1:T(8,128)S(1)} %select_maximum_fusion.1), kind=kLoop, calls=%fused_computation.26 | loop fusion | flops 2621440 | bytes 14680064 | tf_op jit(solution)/shard_map/add | solution.py:17
  89.9 0.8 multiply_subtract_fusion.4
  90.7 2.4 select_maximum_fusion
  93.0 3.5 %slice_add_fusion = f32[8,2,16,16,128]{4,3,2,0,1:T(8,128)S(1)} fusion(f32[8,2,18,18,130]{4,3,2,0,1:T(8,128)S(1)} %select_maximum_fusion), kind=kLoop, calls=%fused_computation.21 | loop fusion | flops 2621440 | bytes 14680064 | tf_op jit(solution)/shard_map/add | solution.py:17
  96.6 0.9 multiply_subtract_fusion.1
  97.5 0.5 multiply_subtract_fusion
  98.0 0.4 maximum_bitcast_fusion
  98.5 0.4 pad_maximum_fusion
  98.9 0.6 copy.17
  99.5 51.6 %all_to_all.36 = f32[2,2,8,16,16,128]{5,4,2,1,0,3:T(8,128)S(1)} all-to-all(f32[2,2,8,16,16,128]{5,4,2,1,0,3:T(8,128)S(1)} %copy.17), channel_id=1, replica_groups=mesh['node'=4,'dom'=8] {'dom'}, dimensions={3} | all-to-all | bytes 8388608 | tf_op jit(solution)/shard_map/all_to_all | solution.py:84
  151.1 0.5 copy.19
  151.7 0.5 bitcast_reduce_fusion
  152.2 0.0 copy-start
  152.2 1.6 collective-permute-start
  153.8 45.2 %collective-permute-done = f32[2,2,32,2,16,128]{5,4,3,2,1,0:T(8,128)S(1)} collective-permute-done((f32[2,2,32,2,16,128]{5,4,3,2,1,0:T(8,128)S(1)}, f32[2,2,32,2,16,128]{5,4,3,2,1,0:T(8,128)S(1)}, u32[]{:S(2)}, u32[]{:S(2)}) %collective-permute-start) | collective-permute-done | bytes 2097184 | tf_op jit(solution)/shard_map/ppermute | solution.py:99
  199.1 1.8 add.646
  200.9 2.6 collective-permute-start.1
  203.5 3.1 fusion.10
  206.6 108.5 %psum.7 = f32[2,2,32,32]{3,2,1,0:T(8,128)} all-reduce(f32[2,2,32,32]{3,2,1,0:T(8,128)S(1)} %fusion.10), channel_id=1, replica_groups=mesh['node'=4,'dom'=8] {'node','dom'}, use_global_device_ids=true, to_apply=%region_1.2 | all-reduce | flops 4096 | bytes 32768 | tf_op jit(solution)/shard_map/psum | solution.py:96
  315.1 0.0 collective-permute-done.1
  315.1 2.1 dynamic-slice_add_fusion
  (9 shorter events, 0.1 us)
Async XLA Ops:
  0.6 7.4 %copy-start.1 = (f32[2,16,128]{2,1,0:T(8,128)S(1)}, f32[2,16,128]{2,1,0:T(8,128)}, u32[]{:S(2)}) copy-start(f32[2,16,128]{2,1,0:T(8,128)} %param.5) | copy-start | bytes 49156
  0.6 26.2 %copy-start.2 = (f32[2,16,128]{2,1,0:T(8,128)S(1)}, f32[2,16,128]{2,1,0:T(8,128)}, u32[]{:S(2)}) copy-start(f32[2,16,128]{2,1,0:T(8,128)} %param.6) | copy-start | bytes 49156
  0.7 34.5 %copy-start.3 = (f32[2,16,128]{2,1,0:T(8,128)S(1)}, f32[2,16,128]{2,1,0:T(8,128)}, u32[]{:S(2)}) copy-start(f32[2,16,128]{2,1,0:T(8,128)} %param.7) | copy-start | bytes 49156
  2.8 41.5 %all-to-all-start = ((f32[64,2,16,128]{3,2,1,0:T(8,128)}), f32[64,2,16,128]{3,2,1,0:T(8,128)S(1)}, u32[]{:S(2)}, u32[]{:S(2)}) async-start(f32[64,2,16,128]{3,2,1,0:T(8,128)} %bitcast), calls=%async_computation | async-start | bytes 2097152 | tf_op jit(solution)/shard_map/all_to_all | solution.py:58
  152.2 51.3 %copy-start = (f32[32,2,16,128]{3,2,1,0:T(8,128)S(1)}, f32[32,2,16,128]{3,2,1,0:T(8,128)}, u32[]{:S(2)}) copy-start(f32[32,2,16,128]{3,2,1,0:T(8,128)} %param.4) | copy-start | bytes 1572868
  152.2 46.9 %collective-permute-start = (f32[2,2,32,2,16,128]{5,4,3,2,1,0:T(8,128)S(1)}, f32[2,2,32,2,16,128]{5,4,3,2,1,0:T(8,128)S(1)}, u32[]{:S(2)}, u32[]{:S(2)}) collective-permute-start(f32[2,2,32,2,16,128]{5,4,3,2,1,0:T(8,128)S(1)} %bitcast_reduce_fusion), channel_id=1, source_target_pairs={{0,8},{8,0},{16,24},{24,16},{1,9},{9,1},{17,25},{25,17},{2,10},{10... | collective-permute-start | bytes 6291464 | tf_op jit(solution)/shard_map/ppermute | solution.py:99
  200.9 114.2 %collective-permute-start.1 = (f32[2,2,32,2,16,128]{5,4,3,2,1,0:T(8,128)}, f32[2,2,32,2,16,128]{5,4,3,2,1,0:T(8,128)}, u32[]{:S(2)}, u32[]{:S(2)}) collective-permute-start(f32[2,2,32,2,16,128]{5,4,3,2,1,0:T(8,128)} %add.646), channel_id=1, source_target_pairs={{0,16},{8,24},{16,0},{24,8},{1,17},{9,25},{17,1},{25,9},{2,18},{10... | collective-permute-start | bytes 6291464 | tf_op jit(solution)/shard_map/ppermute | solution.py:99
